TPU v7x, 32 devices: a whole 2x2x4 slice. The times are simulated.
32 devices in a mesh: parts: 2 (over y), tm: 4 (over z), rows: 2 (over x), cols: 2 (over core).
Axes of the slice: x: 2, y: 2, z: 4, core: 2. Of those that a mesh axis runs over, the one named last changes fastest.
Arguments:
- frames: bfloat16 [256, 256, 512], P(('parts', 'tm'), 'rows', 'cols'), parts along dimension 0, may hold values from -6 to 6
- transfer: bfloat16 [256, 128, 128], P(('parts', 'tm')), parts along dimension 0, may hold values from 0.099609375 to 1
- cutoff: int32 [128, 128], replicated, may hold values from 0 to 64
Outputs:
- restored: float32 [256, 256, 512], P(('parts', 'tm'), 'rows', 'cols'), parts along dimension 0
There are 2 independent parts, one for each index of `parts`. A program takes and returns all parts, laid end to end along the dimension named above; an argument that names none is the same for every part. Nothing has to cross between parts.
Inputs may be any that keep to these rules, and one draw needn't show every extreme that they name: cutoff[u, v] is the largest value of min(w, 128 - w) kept at wavenumber (u, v).
All inputs are finite; a program needn't handle non-finite values.
Results may differ from a plain program's by a relative error of at most 0.0003.
Values may be sent and summed in bfloat16 or wider, within the bound.
No kernel may reach another device: no remote copies, remote signals or barrier semaphores. Data moves between devices by JAX's collectives and lax.ppermute only.
A program may use at most 128 MiB of HBM per device.

v0:
```python
import math
import jax
import jax.numpy as jnp
from jax import lax
from jax.sharding import PartitionSpec as P

noise_level = 0.05


def with_halo(cells, sides, width):
    for axis, dim in sides:
        count = lax.axis_size(axis)
        ends = count - 1
        head = lax.slice_in_dim(cells, 0, width, axis=dim)
        tail = lax.slice_in_dim(cells, cells.shape[dim] - width, cells.shape[dim], axis=dim)
        cells = jnp.concatenate(
            [
                lax.ppermute(tail, axis, [(i, (i + 1) % count) for i in range(ends)]),
                cells,
                lax.ppermute(head, axis, [((i + 1) % count, i) for i in range(ends)]),
            ],
            axis=dim,
        )
    return cells


def tables(length):
    series = jnp.arange(length, dtype=jnp.int32)
    product = series[:, None] * series[None, :] % length
    angles = product.astype(jnp.float32) * (2.0 * math.pi / length)
    return (jnp.cos(angles), jnp.sin(angles))


def forward_spatial(images, cos_space, sin_space):
    highest = lax.Precision.HIGHEST
    factor = 1.0 / cos_space.shape[0]
    row_real = jnp.einsum("cnab,bv->cnav", images, cos_space, precision=highest)
    row_imag = -jnp.einsum("cnab,bv->cnav", images, sin_space, precision=highest)
    spec_real = (
        jnp.einsum("ua,cnav->cnuv", cos_space, row_real, precision=highest)
        + jnp.einsum("ua,cnav->cnuv", sin_space, row_imag, precision=highest)
    ) * factor
    spec_imag = (
        jnp.einsum("ua,cnav->cnuv", cos_space, row_imag, precision=highest)
        - jnp.einsum("ua,cnav->cnuv", sin_space, row_real, precision=highest)
    ) * factor
    return (spec_real, spec_imag)


def inverse_spatial(spec_real, spec_imag, cos_space, sin_space):
    highest = lax.Precision.HIGHEST
    factor = 1.0 / cos_space.shape[0]
    col_real = jnp.einsum("au,cnuv->cnav", cos_space, spec_real, precision=highest) - jnp.einsum(
        "au,cnuv->cnav", sin_space, spec_imag, precision=highest
    )
    col_imag = jnp.einsum("au,cnuv->cnav", cos_space, spec_imag, precision=highest) + jnp.einsum(
        "au,cnuv->cnav", sin_space, spec_real, precision=highest
    )
    return (
        jnp.einsum("cnav,vb->cnab", col_real, cos_space, precision=highest)
        - jnp.einsum("cnav,vb->cnab", col_imag, sin_space, precision=highest)
    ) * factor


def join(spec_real, spec_imag, gains, count):
    numerator_real = jnp.zeros(spec_real.shape[:1] + (count,) + spec_real.shape[2:], jnp.float32)
    numerator_imag = jnp.zeros_like(numerator_real)
    denominator = jnp.zeros(gains.shape[:1] + (count,) + gains.shape[2:], jnp.float32)
    for offset in range(5):
        gain = lax.slice_in_dim(gains, offset, offset + count, axis=1)
        numerator_real = numerator_real + gain * lax.slice_in_dim(
            spec_real, offset, offset + count, axis=1
        )
        numerator_imag = numerator_imag + gain * lax.slice_in_dim(
            spec_imag, offset, offset + count, axis=1
        )
        denominator = denominator + gain * gain
    denominator = denominator + noise_level
    return (numerator_real / denominator, numerator_imag / denominator)


def temporal(stacked, cutoff_local, channels):
    highest = lax.Precision.HIGHEST
    time_len = stacked.shape[1]
    cos_time, sin_time = tables(time_len)
    factor = 1.0 / math.sqrt(time_len)
    real = stacked[:channels]
    imag = stacked[channels:]
    freq_real = (
        jnp.einsum("wt,stk->swk", cos_time, real, precision=highest)
        + jnp.einsum("wt,stk->swk", sin_time, imag, precision=highest)
    ) * factor
    freq_imag = (
        jnp.einsum("wt,stk->swk", cos_time, imag, precision=highest)
        - jnp.einsum("wt,stk->swk", sin_time, real, precision=highest)
    ) * factor
    omega = jnp.arange(time_len, dtype=jnp.int32)
    distance = jnp.minimum(omega, time_len - omega)
    keeper = (distance[:, None] <= cutoff_local[None, :])[None]
    freq_real = jnp.where(keeper, freq_real, 0.0)
    freq_imag = jnp.where(keeper, freq_imag, 0.0)
    back_real = (
        jnp.einsum("tw,swk->stk", cos_time, freq_real, precision=highest)
        - jnp.einsum("tw,swk->stk", sin_time, freq_imag, precision=highest)
    ) * factor
    back_imag = (
        jnp.einsum("tw,swk->stk", cos_time, freq_imag, precision=highest)
        + jnp.einsum("tw,swk->stk", sin_time, freq_real, precision=highest)
    ) * factor
    return jnp.concatenate([back_real, back_imag], axis=0)


def to_channels(images, side, across):
    total = images.shape[0]
    return images.reshape(total, side, across, side).transpose(2, 0, 1, 3)


def on_device(frames, transfer, cutoff):
    count = frames.shape[0]
    side = transfer.shape[1]
    across = frames.shape[2] // side
    cos_space, sin_space = tables(side)
    packed = jnp.concatenate([frames, transfer], axis=2)
    extended = with_halo(packed, (("tm", 0),), 2)
    images = to_channels(extended[:, :, : across * side].astype(jnp.float32), side, across)
    spec_real, spec_imag = forward_spatial(images, cos_space, sin_space)
    gains = extended[:, :, across * side :].astype(jnp.float32)[None]
    joined_real, joined_imag = join(spec_real, spec_imag, gains, count)
    payload = jnp.concatenate([joined_real, joined_imag], axis=0).reshape(
        2 * across, count, side * side
    )
    gathered = lax.all_to_all(payload, "tm", split_axis=2, concat_axis=1, tiled=True)
    width = gathered.shape[2]
    start = lax.axis_index("tm") * width
    cutoff_local = lax.dynamic_slice_in_dim(cutoff.reshape(-1), start, width)
    filtered = temporal(gathered, cutoff_local, across)
    returned = lax.all_to_all(filtered, "tm", split_axis=1, concat_axis=2, tiled=True)
    spectra_back = returned.reshape(2 * across, count, side, side)
    result = inverse_spatial(spectra_back[:across], spectra_back[across:], cos_space, sin_space)
    return result.transpose(1, 2, 0, 3).reshape(count, side, across * side)


def solution(mesh):
    return jax.shard_map(
        on_device,
        mesh=mesh,
        in_specs=(P(("parts", "tm"), "rows", "cols"), P(("parts", "tm"), None, None), P()),
        out_specs=P(("parts", "tm"), "rows", "cols"),
        check_vma=False,
    )
```

profile of v0, /device:TPU:0, one launch (start us, length us, event | category | flops | bytes accessed | tf_op | source)
XLA Modules:
  0.0 778.8 jit_solution(10579485411199657045)
XLA Ops:
  0.0 3.2 copy.61
  3.2 0.0 copy-start.2
  3.2 2.2 copy.62
  5.5 0.0 copy-start.5
  5.5 5.0 collective-permute-start
  10.5 1.3 collective-permute-start.1
  11.8 2.8 collective-permute-done
  14.6 4.1 collective-permute-done.1
  18.8 1.6 pad_maximum_fusion.2
  20.3 0.0 copy-done.2
  20.3 0.0 copy-done.5
  20.3 3.0 copy.63
  23.4 2.3 fusion.30
  25.7 2.2 fusion.32
  27.9 7.9 %fusion.10 = f32[2,36,128,128]{3,2,1,0:T(8,128)S(1)} fusion(f32[2,36,128,128]{3,2,1,0:T(8,128)S(1)} %fusion.30), kind=kOutput, calls=%fused_computation.18 | convolution fusion | flops 1813348352 | bytes 9437184 | tf_op jit(solution)/shard_map/ua,cnav->cnuv/dot_general | solution.py:44
  35.8 7.7 fusion.12
  43.5 4.8 multiply_bitcast_fusion
  48.3 0.0 copy-start.3
  48.3 0.0 copy-start.6
  48.3 4.4 multiply_bitcast_fusion.1
  52.7 1.7 fusion.36
  54.4 11.6 %slice_bitcast_fusion.4 = (f32[32,128,128]{1,2,0:T(8,128)}, f32[32,128,128]{1,2,0:T(8,128)}, f32[32,128,128]{1,2,0:T(8,128)}, f32[32,128,128]{1,2,0:T(8,128)}, f...) fusion(f32[1,36,128,128]{2,3,1,0:T(8,128)} %fusion.36), kind=kLoop, calls=%fused_computation.61 | loop fusion | flops 5242880 | bytes 23068672 | tf_op jit(solution)/shard_map/mul | solution.py:71
  66.0 9.8 %fusion.20 = (f32[2,32,128,128]{2,3,1,0:T(8,128)S(1)}, f32[2,32,128,128]{2,3,1,0:T(8,128)}) fusion(f32[2,36,128,128]{2,3,1,0:T(8,128)S(1)} %multiply_bitcast_fusion.1, f32[32,128,128]{1,2,0:T(8,128)} %get-tuple-element.14, f32[32,128,128]{1,2,0:T(8,128)} %get-tuple-element.15, f32[32,128,128]{1,2,0:T(8,128)} %get-tuple-element.16, ...), kind=kLoop, calls=%fused_computation.34 | loop fusion | flops 20971520 | bytes 62914560 | tf_op jit(solution)/shard_map/div | solution.py:79
  75.8 6.2 pad_maximum_fusion
  82.0 26.7 %copy.146 = f32[4,32,128,128]{1,0,3,2:T(4,128)} copy(f32[4,32,128,128]{2,3,1,0:T(8,128)} %pad_maximum_fusion) | data formatting | bytes 16777216 | tf_op jit(solution)/shard_map/reshape | solution.py:129
  108.7 41.7 %reshape.77 = f32[4,1,524288]{2,1,0:T(1,128)} reshape(f32[16384,4,32]{2,1,0:T(4,128)} %bitcast.139) | data formatting | bytes 16777216
  150.4 5.6 all-to-all-start
  156.1 0.7 dynamic_slice.3
  156.8 1.8 broadcast_compare_fusion
  158.7 179.6 %all-to-all-done = f32[4,1,524288]{2,1,0:T(1,128)} async-done(((f32[4,1,524288]{2,1,0:T(1,128)}), f32[4,1,524288]{2,1,0:T(1,128)}, u32[]{:S(2)}, u32[]{:S(2)}) %all-to-all-start) | async-done | bytes 8388640 | tf_op jit(solution)/shard_map/all_to_all | solution.py:132
  338.3 0.5 broadcast.190
  338.8 28.4 %reduce = f32[4,524288]{1,0:T(4,128)} reduce(f32[4,1,524288]{2,1,0:T(1,128)} %all-to-all-done, f32[]{:T(128)} %broadcast.190), dimensions={1}, to_apply=%all_to_all.22.reduce_sub_computation | reduce | bytes 16777220 | tf_op jit(solution)/shard_map/all_to_all | solution.py:132
  367.2 47.7 %reshape.78 = f32[16384,4,32]{2,1,0:T(4,128)} reshape(f32[4,524288]{1,0:T(4,128)} %reduce) | data formatting | bytes 16777216
  415.0 28.8 %copy.147 = f32[4,32,4,4096]{3,2,1,0:T(4,128)} copy(f32[4,32,4,4096]{1,0,3,2:T(4,128)} %bitcast.140) | data formatting | bytes 16777216 | tf_op jit(solution)/shard_map/all_to_all | solution.py:132
  443.8 4.0 fusion.174
  447.9 2.4 copy.77
  450.3 6.8 fusion.50
  457.1 2.6 copy.80
  459.8 6.8 fusion.46
  466.6 7.3 fusion.9
  473.9 3.7 fusion.48
  477.5 7.0 fusion.6
  484.6 3.7 fusion.44
  488.2 3.7 fusion.3
  491.9 4.1 fusion.1
  496.0 3.8 pad_maximum_fusion.1
  499.8 10.3 %copy.91 = f32[4,128,4096]{2,0,1:T(4,128)} copy(f32[4,128,4096]{1,2,0:T(8,128)} %pad_maximum_fusion.1) | data formatting | bytes 16777216 | tf_op jit(solution)/shard_map/concatenate | solution.py:110
  510.1 186.7 %all_to_all.30 = f32[4,128,4096]{2,0,1:T(4,128)S(1)} all-to-all(f32[4,128,4096]{2,0,1:T(4,128)} %copy.91), channel_id=1, replica_groups=mesh['parts'=2,'tm'=4,'rows'=2,'cols'=2] {'tm'}, dimensions={1} | all-to-all | bytes 16777216 | tf_op jit(solution)/shard_map/all_to_all | solution.py:137
  696.7 4.9 copy.92
  701.6 2.8 fusion.173
  704.4 4.7 copy.96
  709.0 6.1 slice.107
  715.1 10.3 %fusion.61 = f32[2,32,128,128]{3,2,1,0:T(8,128)} fusion(f32[2,32,128,128]{3,2,1,0:T(8,128)} %slice.107), kind=kOutput, calls=%fused_computation.94 | convolution fusion | flops 1610842112 | bytes 8388608 | tf_op jit(solution)/shard_map/au,cnuv->cnav/dot_general | solution.py:56
  725.5 8.6 %fusion.55 = f32[2,32,128,128]{3,2,1,0:T(8,128)} fusion(f32[2,32,128,128]{3,2,1,0:T(8,128)S(1)} %copy-done), kind=kOutput, calls=%fused_computation.88 | convolution fusion | flops 1610842112 | bytes 8388608 | tf_op jit(solution)/shard_map/au,cnuv->cnav/dot_general | solution.py:53
  734.1 4.7 copy.93
  738.8 6.1 slice.105
  744.9 9.3 %fusion.53 = f32[2,32,128,128]{3,2,1,0:T(8,128)S(1)} fusion(f32[2,32,128,128]{3,2,1,0:T(8,128)} %slice.105), kind=kOutput, calls=%fused_computation.86 | convolution fusion | flops 1610842112 | bytes 8388608 | tf_op jit(solution)/shard_map/au,cnuv->cnav/dot_general | solution.py:56
  754.2 7.0 fusion.63
  761.2 0.0 copy-done.4
  761.2 0.0 copy-start.7
  761.2 4.3 fusion.24
  765.6 4.9 multiply_bitcast_fusion.2
  770.5 2.2 copy.105
  772.7 5.6 copy.106
  (12 shorter events, 0.1 us)
Async XLA Ops:
  3.2 17.1 %copy-start.2 = (bf16[32,128,256]{1,2,0:T(8,128)(2,1)}, bf16[32,128,256]{1,2,0:T(8,128)(2,1)S(1)}, u32[]{:S(2)}) copy-start(bf16[32,128,256]{1,2,0:T(8,128)(2,1)S(1)} %copy.61) | copy-start | bytes 6291460
  5.5 14.8 %copy-start.5 = (bf16[32,128,128]{1,2,0:T(8,128)(2,1)}, bf16[32,128,128]{1,2,0:T(8,128)(2,1)S(1)}, u32[]{:S(2)}) copy-start(bf16[32,128,128]{1,2,0:T(8,128)(2,1)S(1)} %copy.62) | copy-start | bytes 3145732
  5.5 9.1 %collective-permute-start = (bf16[2,128,384]{1,2,0:T(8,128)(2,1)S(1)}, bf16[2,128,384]{1,2,0:T(8,128)(2,1)S(1)}, u32[]{:S(2)}, u32[]{:S(2)}) collective-permute-start(bf16[2,128,384]{1,2,0:T(8,128)(2,1)S(1)} %get-tuple-element.11), channel_id=1, source_target_pairs={{0,4},{4,8},{8,12},{1,5},{5,9},{9,13},{2,6},{6,10},{10,14},{3,7},{... | collective-permute-start | bytes 589832 | tf_op jit(solution)/shard_map/ppermute | solution.py:18
  10.5 8.3 %collective-permute-start.1 = (bf16[2,128,384]{1,2,0:T(8,128)(2,1)S(1)}, bf16[2,128,384]{1,2,0:T(8,128)(2,1)S(1)}, u32[]{:S(2)}, u32[]{:S(2)}) collective-permute-start(bf16[2,128,384]{1,2,0:T(8,128)(2,1)S(1)} %get-tuple-element.12), channel_id=1, source_target_pairs={{4,0},{8,4},{12,8},{5,1},{9,5},{13,9},{6,2},{10,6},{14,10},{7,3},{... | collective-permute-start | bytes 589832 | tf_op jit(solution)/shard_map/ppermute | solution.py:20
  48.3 4.4 copy-start.3
  48.3 4.4 copy-start.6
  150.4 187.9 %all-to-all-start = ((f32[4,1,524288]{2,1,0:T(1,128)}), f32[4,1,524288]{2,1,0:T(1,128)}, u32[]{:S(2)}, u32[]{:S(2)}) async-start(f32[4,1,524288]{2,1,0:T(1,128)} %reshape.77), calls=%async_computation | async-start | bytes 16777216 | tf_op jit(solution)/shard_map/all_to_all | solution.py:132
  715.1 10.4 %copy-start = (f32[2,32,128,128]{3,2,1,0:T(8,128)S(1)}, f32[2,32,128,128]{3,2,1,0:T(8,128)}, u32[]{:S(2)}) copy-start(f32[2,32,128,128]{3,2,1,0:T(8,128)} %slice.107) | copy-start | bytes 12582916
  725.5 8.7 %copy-start.8 = (f32[2,32,4,4096]{3,1,2,0:T(8,128)S(1)}, f32[2,32,4,4096]{3,1,2,0:T(8,128)}, u32[]{:S(2)}) copy-start(f32[2,32,4,4096]{3,1,2,0:T(8,128)} %get-tuple-element.7) | copy-start | bytes 12582916
  744.9 9.3 %copy-start.1 = (f32[2,32,128,128]{3,2,1,0:T(8,128)S(1)}, f32[2,32,128,128]{3,2,1,0:T(8,128)}, u32[]{:S(2)}) copy-start(f32[2,32,128,128]{3,2,1,0:T(8,128)} %slice.105) | copy-start | bytes 12582916
  754.2 7.1 copy-start.4
  761.2 4.3 copy-start.7
where the time goes:
time: 790 us; the launch traced here: 779 us
  local copies, waits for them, and re-layouts  211 us (27%)
  waiting for transfers between devices  187 us (24%)
  blocking collectives  187 us (24%)
  matrix products  117 us (15%)
  other arithmetic  64.9 us (8%)
  starting transfers between devices  11.9 us (2%)
    all_to_all x1, blocking collectives, on_device(): lax.all_to_all(filtered, 'tm', split_axis=1, concat_axis=2, tiled=True)  187 us
    all_to_all x1, waiting for transfers between devices, on_device(): lax.all_to_all(payload, 'tm', split_axis=2, concat_axis=1, tiled=True)  180 us
    unnamed x22, local copies, waits for them, and re-layouts  94.9 us
    all_to_all x2, local copies, waits for them, and re-layouts, on_device(): lax.all_to_all(payload, 'tm', split_axis=2, concat_axis=1, tiled=True)  29.4 us
    all_to_all x1, other arithmetic, on_device(): lax.all_to_all(payload, 'tm', split_axis=2, concat_axis=1, tiled=True)  28.4 us
    reshape x1, local copies, waits for them, and re-layouts, on_device(): jnp.concatenate([joined_real, joined_imag], axis=0)  26.7 us
  transfers between devices with their start and end apart: 3, of which 3 were waited for; matrix products, arithmetic and copies ran while one was open for 0% of the time, Pallas kernels for 0%

commit v1 on v0

--- a/solution.py
+++ b/solution.py
@@ -129,7 +129,10 @@
     payload = jnp.concatenate([joined_real, joined_imag], axis=0).reshape(
         2 * across, count, side * side
     )
-    gathered = lax.all_to_all(payload, "tm", split_axis=2, concat_axis=1, tiled=True)
+    gathered = jnp.concatenate(
+        lax.all_to_all(jnp.stack(jnp.split(payload, lax.axis_size("tm"), axis=2)), "tm", 0, 0),
+        axis=1,
+    )
     width = gathered.shape[2]
     start = lax.axis_index("tm") * width
     cutoff_local = lax.dynamic_slice_in_dim(cutoff.reshape(-1), start, width)

time: 790 us -> 637 us (0.81)
  local copies, waits for them, and re-layouts: 211 us -> 83.8 us
  other arithmetic: 64.9 us -> 40.4 us
    unnamed x22 -> x20, local copies, waits for them, and re-layouts: 94.9 us -> 5.5 us
    all_to_all x2 -> x0, local copies, waits for them, and re-layouts: 29.4 us -> none  [on_device(): lax.all_to_all(payload, 'tm', split_axis=2, concat_axis=1, tiled=True)]
    all_to_all x1 -> x0, other arithmetic: 28.4 us -> none  [on_device(): lax.all_to_all(payload, 'tm', split_axis=2, concat_axis=1, tiled=True)]
    reshape x1, local copies, waits for them, and re-layouts: 26.7 us -> 9.37 us  [on_device(): jnp.concatenate([joined_real, joined_imag], axis=0)]
    concatenate x0 -> x1, local copies, waits for them, and re-layouts: none -> 8.99 us  [on_device(): jnp.concatenate([joined_real, joined_imag], axis=0)]
where the time goes in v1:
time: 637 us; the launch traced here: 627 us
  blocking collectives  187 us (29%)
  waiting for transfers between devices  186 us (29%)
  matrix products  117 us (18%)
  local copies, waits for them, and re-layouts  83.8 us (13%)
  other arithmetic  40.4 us (6%)
  starting transfers between devices  11.9 us (2%)
    all_to_all x1, blocking collectives, on_device(): lax.all_to_all(filtered, 'tm', split_axis=1, concat_axis=2, tiled=True)  187 us
    all_to_all x1, waiting for transfers between devices, on_device(): lax.all_to_all(jnp.stack(jnp.split(payload, lax.axis_size('tm'), axis=2))...  179 us
    slice x3, local copies, waits for them, and re-layouts, on_device(): spectra_back[:across]  13.5 us
  transfers between devices with their start and end apart: 3, of which 3 were waited for; matrix products, arithmetic and copies ran while one was open for 0% of the time, Pallas kernels for 0%

profile of v1, /device:TPU:0, one launch (start us, length us, event | category | flops | bytes accessed | tf_op | source)
XLA Modules:
  0.0 626.9 jit_solution(2504989434783784409)
XLA Ops:
  0.0 3.2 copy.64
  3.2 0.0 copy-start.2
  3.2 2.2 copy.65
  5.5 0.0 copy-start.5
  5.5 5.0 collective-permute-start
  10.5 1.3 collective-permute-start.1
  11.8 2.8 collective-permute-done
  14.6 4.1 collective-permute-done.1
  18.8 1.6 pad_maximum_fusion.3
  20.3 0.0 copy-done.2
  20.3 0.0 copy-done.5
  20.3 3.0 copy.66
  23.4 2.3 fusion.30
  25.7 2.2 fusion.32
  27.9 8.0 %fusion.10 = f32[2,36,128,128]{3,2,1,0:T(8,128)S(1)} fusion(f32[2,36,128,128]{3,2,1,0:T(8,128)S(1)} %fusion.30), kind=kOutput, calls=%fused_computation.19 | convolution fusion | flops 1813348352 | bytes 9437184 | tf_op jit(solution)/shard_map/ua,cnav->cnuv/dot_general | solution.py:44
  36.0 7.7 %fusion.12 = f32[2,36,128,128]{3,2,1,0:T(8,128)S(1)} fusion(f32[2,36,128,128]{3,2,1,0:T(8,128)S(1)} %fusion.30), kind=kOutput, calls=%fused_computation.21 | convolution fusion | flops 1813348352 | bytes 9437184 | tf_op jit(solution)/shard_map/ua,cnav->cnuv/dot_general | solution.py:41
  43.6 4.5 multiply_bitcast_fusion
  48.2 0.0 copy-start.3
  48.2 4.4 multiply_bitcast_fusion.1
  52.6 0.0 copy-done.3
  52.6 0.0 copy-done.6
  52.6 1.7 fusion.36
  54.3 11.7 %slice_bitcast_fusion.8 = (f32[32,128,128]{1,2,0:T(8,128)}, f32[32,128,128]{1,2,0:T(8,128)}, f32[32,128,128]{1,2,0:T(8,128)}, f32[32,128,128]{1,2,0:T(8,128)}, f...) fusion(f32[1,36,128,128]{2,3,1,0:T(8,128)} %fusion.36), kind=kLoop, calls=%fused_computation.66 | loop fusion | flops 5242880 | bytes 23068672 | tf_op jit(solution)/shard_map/mul | solution.py:71
  65.9 9.8 %fusion.20 = (f32[2,32,128,128]{2,3,1,0:T(8,128)S(1)}, f32[2,32,128,128]{2,3,1,0:T(8,128)}) fusion(f32[2,36,128,128]{2,3,1,0:T(8,128)S(1)} %multiply_bitcast_fusion.1, f32[32,128,128]{1,2,0:T(8,128)} %get-tuple-element.18, f32[32,128,128]{1,2,0:T(8,128)} %get-tuple-element.19, f32[32,128,128]{1,2,0:T(8,128)} %get-tuple-element.20, ...), kind=kLoop, calls=%fused_computation.35 | loop fusion | flops 20971520 | bytes 62914560 | tf_op jit(solution)/shard_map/div | solution.py:79
  75.8 6.3 pad_maximum_fusion
  82.0 9.0 %copy.77 = f32[4,32,128,128]{3,2,1,0:T(8,128)} copy(f32[4,32,128,128]{2,3,1,0:T(8,128)} %pad_maximum_fusion) | data formatting | bytes 16777216 | tf_op jit(solution)/shard_map/concatenate | solution.py:129
  91.0 9.4 %reshape.58 = f32[4,32,16384]{2,1,0:T(8,128)} reshape(f32[4,32,128,128]{3,2,1,0:T(8,128)} %copy.77) | data formatting | bytes 16777216 | tf_op jit(solution)/shard_map/reshape | solution.py:129
  100.4 4.0 slice_bitcast_fusion.3
  104.4 3.6 pad_maximum_fusion.1
  108.0 5.6 all-to-all-start
  113.6 0.7 dynamic_slice.3
  114.4 2.1 broadcast_compare_fusion
  116.4 179.4 %all-to-all-done = f32[4,4,32,4096]{3,2,1,0:T(8,128)} async-done(((f32[4,4,32,4096]{3,2,1,0:T(8,128)}), f32[4,4,32,4096]{3,2,1,0:T(8,128)}, u32[]{:S(2)}, u32[]{:S(2)}) %all-to-all-start) | async-done | bytes 8388640 | tf_op jit(solution)/shard_map/all_to_all | solution.py:133
  295.9 4.0 fusion.174
  299.9 0.4 copy.78
  300.3 6.8 %fusion.50 = f32[2,4096,128]{2,1,0:T(8,128)S(1)} fusion(f32[2,128,4096]{2,1,0:T(8,128)S(1)} %bitcast.145), kind=kOutput, calls=%fused_computation.88 | convolution fusion | flops 1610842112 | bytes 8388608 | tf_op jit(solution)/shard_map/wt,stk->swk/dot_general | solution.py:90
  307.1 0.4 copy.81
  307.6 7.2 %fusion.46 = f32[2,4096,128]{2,1,0:T(8,128)S(1)} fusion(f32[2,128,4096]{2,1,0:T(8,128)S(1)} %bitcast.147), kind=kOutput, calls=%fused_computation.84 | convolution fusion | flops 1610842112 | bytes 8388608 | tf_op jit(solution)/shard_map/wt,stk->swk/dot_general | solution.py:94
  314.8 6.9 %fusion.9 = f32[2,128,4096]{1,2,0:T(8,128)S(1)} fusion(f32[2,4096,128]{2,1,0:T(8,128)S(1)} %fusion.50, f32[2,128,4096]{2,1,0:T(8,128)S(1)} %bitcast.148, pred[128,4096]{0,1:T(8,128)(4,1)S(1)} %broadcast_compare_fusion), kind=kOutput, calls=%fused_computation.16 | convolution fusion | flops 1613987840 | bytes 13107200 | tf_op jit(solution)/shard_map/wt,stk->swk/dot_general | solution.py:91
  321.7 3.8 fusion.48
  325.5 6.9 %fusion.6 = f32[2,128,4096]{1,2,0:T(8,128)S(1)} fusion(f32[2,4096,128]{2,1,0:T(8,128)S(1)} %fusion.46, f32[2,128,4096]{2,1,0:T(8,128)S(1)} %bitcast.146, pred[128,4096]{0,1:T(8,128)(4,1)S(1)} %broadcast_compare_fusion), kind=kOutput, calls=%fused_computation.12 | convolution fusion | flops 1613987840 | bytes 13107200 | tf_op jit(solution)/shard_map/wt,stk->swk/dot_general | solution.py:95
  332.4 3.9 fusion.44
  336.3 3.7 fusion.3
  340.0 3.7 fusion.1
  343.6 3.8 pad_maximum_fusion.2
  347.4 10.3 %copy.92 = f32[4,128,4096]{2,0,1:T(4,128)} copy(f32[4,128,4096]{1,2,0:T(8,128)} %pad_maximum_fusion.2) | data formatting | bytes 16777216 | tf_op jit(solution)/shard_map/concatenate | solution.py:110
  357.7 187.1 %all_to_all.20 = f32[4,128,4096]{2,0,1:T(4,128)S(1)} all-to-all(f32[4,128,4096]{2,0,1:T(4,128)} %copy.92), channel_id=1, replica_groups=mesh['parts'=2,'tm'=4,'rows'=2,'cols'=2] {'tm'}, dimensions={1} | all-to-all | bytes 16777216 | tf_op jit(solution)/shard_map/all_to_all | solution.py:140
  544.8 4.9 copy.93
  549.6 2.8 fusion.173
  552.4 4.7 copy.97
  557.1 6.1 slice.107
  563.2 10.4 %fusion.61 = f32[2,32,128,128]{3,2,1,0:T(8,128)} fusion(f32[2,32,128,128]{3,2,1,0:T(8,128)} %slice.107), kind=kOutput, calls=%fused_computation.99 | convolution fusion | flops 1610842112 | bytes 8388608 | tf_op jit(solution)/shard_map/au,cnuv->cnav/dot_general | solution.py:56
  573.5 8.7 %fusion.55 = f32[2,32,128,128]{3,2,1,0:T(8,128)} fusion(f32[2,32,128,128]{3,2,1,0:T(8,128)S(1)} %copy-done), kind=kOutput, calls=%fused_computation.93 | convolution fusion | flops 1610842112 | bytes 8388608 | tf_op jit(solution)/shard_map/au,cnuv->cnav/dot_general | solution.py:53
  582.2 4.7 copy.94
  586.9 6.1 slice.105
  593.0 9.3 %fusion.53 = f32[2,32,128,128]{3,2,1,0:T(8,128)S(1)} fusion(f32[2,32,128,128]{3,2,1,0:T(8,128)} %slice.105), kind=kOutput, calls=%fused_computation.91 | convolution fusion | flops 1610842112 | bytes 8388608 | tf_op jit(solution)/shard_map/au,cnuv->cnav/dot_general | solution.py:56
  602.3 7.0 %fusion.63 = f32[2,32,128,128]{3,2,1,0:T(8,128)S(1)} fusion(f32[2,32,128,128]{3,2,1,0:T(8,128)S(1)} %copy-done.1), kind=kOutput, calls=%fused_computation.101 | convolution fusion | flops 1610842112 | bytes 8388608 | tf_op jit(solution)/shard_map/au,cnuv->cnav/dot_general | solution.py:53
  609.3 0.0 copy-done.4
  609.3 0.0 copy-start.7
  609.4 4.3 fusion.24
  613.7 0.0 copy-done.7
  613.7 4.9 multiply_bitcast_fusion.2
  618.6 2.2 copy.106
  620.8 5.6 copy.107
  (10 shorter events, 0.0 us)
Async XLA Ops:
  3.2 17.1 %copy-start.2 = (bf16[32,128,256]{1,2,0:T(8,128)(2,1)}, bf16[32,128,256]{1,2,0:T(8,128)(2,1)S(1)}, u32[]{:S(2)}) copy-start(bf16[32,128,256]{1,2,0:T(8,128)(2,1)S(1)} %copy.64) | copy-start | bytes 6291460
  5.5 14.8 %copy-start.5 = (bf16[32,128,128]{1,2,0:T(8,128)(2,1)}, bf16[32,128,128]{1,2,0:T(8,128)(2,1)S(1)}, u32[]{:S(2)}) copy-start(bf16[32,128,128]{1,2,0:T(8,128)(2,1)S(1)} %copy.65) | copy-start | bytes 3145732
  5.5 9.1 %collective-permute-start = (bf16[2,128,384]{1,2,0:T(8,128)(2,1)S(1)}, bf16[2,128,384]{1,2,0:T(8,128)(2,1)S(1)}, u32[]{:S(2)}, u32[]{:S(2)}) collective-permute-start(bf16[2,128,384]{1,2,0:T(8,128)(2,1)S(1)} %get-tuple-element.15), channel_id=1, source_target_pairs={{0,4},{4,8},{8,12},{1,5},{5,9},{9,13},{2,6},{6,10},{10,14},{3,7},{... | collective-permute-start | bytes 589832 | tf_op jit(solution)/shard_map/ppermute | solution.py:18
  10.5 8.3 %collective-permute-start.1 = (bf16[2,128,384]{1,2,0:T(8,128)(2,1)S(1)}, bf16[2,128,384]{1,2,0:T(8,128)(2,1)S(1)}, u32[]{:S(2)}, u32[]{:S(2)}) collective-permute-start(bf16[2,128,384]{1,2,0:T(8,128)(2,1)S(1)} %get-tuple-element.16), channel_id=1, source_target_pairs={{4,0},{8,4},{12,8},{5,1},{9,5},{13,9},{6,2},{10,6},{14,10},{7,3},{... | collective-permute-start | bytes 589832 | tf_op jit(solution)/shard_map/ppermute | solution.py:20
  48.2 4.4 copy-start.3
  48.2 4.4 copy-start.6
  108.0 187.9 %all-to-all-start = ((f32[4,4,32,4096]{3,2,1,0:T(8,128)}), f32[4,4,32,4096]{3,2,1,0:T(8,128)}, u32[]{:S(2)}, u32[]{:S(2)}) async-start(f32[4,4,32,4096]{3,2,1,0:T(8,128)} %pad_maximum_fusion.1), calls=%async_computation | async-start | bytes 16777216 | tf_op jit(solution)/shard_map/all_to_all | solution.py:133
  563.2 10.4 %copy-start = (f32[2,32,128,128]{3,2,1,0:T(8,128)S(1)}, f32[2,32,128,128]{3,2,1,0:T(8,128)}, u32[]{:S(2)}) copy-start(f32[2,32,128,128]{3,2,1,0:T(8,128)} %slice.107) | copy-start | bytes 12582916
  573.5 8.7 %copy-start.8 = (f32[2,32,4,4096]{3,1,2,0:T(8,128)S(1)}, f32[2,32,4,4096]{3,1,2,0:T(8,128)}, u32[]{:S(2)}) copy-start(f32[2,32,4,4096]{3,1,2,0:T(8,128)} %get-tuple-element.7) | copy-start | bytes 12582916
  593.0 9.3 %copy-start.1 = (f32[2,32,128,128]{3,2,1,0:T(8,128)S(1)}, f32[2,32,128,128]{3,2,1,0:T(8,128)}, u32[]{:S(2)}) copy-start(f32[2,32,128,128]{3,2,1,0:T(8,128)} %slice.105) | copy-start | bytes 12582916
  602.3 7.1 %copy-start.4 = (f32[2,32,128,128]{3,2,1,0:T(8,128)S(1)}, f32[2,32,128,128]{3,2,1,0:T(8,128)}, u32[]{:S(2)}) copy-start(f32[2,32,128,128]{3,2,1,0:T(8,128)} %fusion.61) | copy-start | bytes 12582916
  609.3 4.4 copy-start.7
